TPU v7x, 32 devices: a whole 2x2x4 slice. The times are simulated.
32 devices in a mesh: tm: 8 (over y, x, core), sector: 4 (over z).
Axes of the slice: x: 2, y: 2, z: 4, core: 2. Of those that a mesh axis runs over, the one named last changes fastest.
Arguments:
- propagator: bfloat16 [4, 8, 640, 640], P('sector', 'tm'), may hold values from -6 to 6
- rising_op: bfloat16 [4, 640, 640], P('sector'), may hold values from -0.25 to 0.25
- energies: float32 [4, 640], P('sector'), may hold values from 0.5 to 40
- hyb_particle: float32 [8], P('tm'), may hold values from 0.2 to 1
- hyb_hole: float32 [8], P('tm'), may hold values from 0.2 to 1
- sector_sizes: int32 [4], P('sector'), may hold values from 160 to 640, as said below
Outputs:
- new_prop: bfloat16 [4, 8, 640, 640], P('sector', 'tm')
Inputs may be any that keep to these rules, and one draw needn't show every extreme that they name: `sector_sizes`: one sector holds exactly 640 states.
All inputs are finite; a program needn't handle non-finite values.
Results may differ from a plain program's by a relative error of at most 0.0061.
Values may be sent and summed in bfloat16 or wider, within the bound.
A program may use at most 128 MiB of HBM per device.

v0:
```python
import functools
import jax
import jax.numpy as jnp
from jax import lax
from jax.experimental import pallas as pl
from jax.experimental.pallas import tpu as pltpu
from jax.sharding import PartitionSpec as P


def shifted(block, axis, distance):
    devices = range(lax.axis_size(axis))
    route = [(i - distance, i) for i in devices if i - distance in devices]
    return lax.ppermute(block, axis, route)


def general_device(propagator, rising_op, energies, hyb_particle, hyb_hole, sector_sizes):
    t_dev = propagator.shape[1]
    states = propagator.shape[2]
    time_count = t_dev * lax.axis_size("tm")
    step_size = 1.0 / time_count
    positions = jnp.arange(states, dtype=jnp.int32)
    live_mask = positions < sector_sizes[0]
    square = live_mask[:, None] & live_mask[None, :]
    masked_prop = jnp.where(square[None], propagator[0], jnp.zeros((), jnp.bfloat16))
    operator = rising_op[0]
    raised = jnp.einsum(
        "ik,tkl->til", operator, masked_prop, preferred_element_type=jnp.float32
    ).astype(jnp.bfloat16)
    upward = jnp.einsum("tik,jk->tij", raised, operator, preferred_element_type=jnp.float32).astype(
        jnp.bfloat16
    )
    from_below = shifted(upward, "sector", 1)
    from_above = shifted(masked_prop, "sector", -1)
    lowered = jnp.einsum(
        "ki,tkl->til", operator, from_above, preferred_element_type=jnp.float32
    ).astype(jnp.bfloat16)
    downward = jnp.einsum("tik,kl->til", lowered, operator, preferred_element_type=jnp.float32)
    combined = (
        hyb_particle[:, None, None] * from_below.astype(jnp.float32)
        + hyb_hole[:, None, None] * downward
    )
    self_energy = jnp.where(square[None], combined, jnp.zeros((), jnp.float32)).astype(jnp.bfloat16)
    rows_each = states // lax.axis_size("tm")
    first_row = lax.axis_index("tm") * rows_each
    lag_rows = lax.all_to_all(self_energy, "tm", split_axis=1, concat_axis=0, tiled=True)
    history = lax.all_gather(masked_prop, "tm", axis=0, tiled=True)
    mirrored = jnp.concatenate([history[::-1], history], 0)
    slots = jnp.arange(time_count, dtype=jnp.int32)
    wide_slots = jnp.arange(time_count + 1, dtype=jnp.int32)

    def pair_step(lag, sums):
        forward, backward = sums
        other = time_count - 1 - lag
        window = lax.dynamic_slice_in_dim(mirrored, lag, time_count + 1, 0)
        near = lax.dynamic_index_in_dim(lag_rows, lag, 0, keepdims=False)
        far = lax.dynamic_index_in_dim(lag_rows, other, 0, keepdims=False)
        left = jnp.where((wide_slots < time_count - lag)[:, None, None], near[None], far[None])
        product = jnp.einsum("uik,ukl->uil", left, window, preferred_element_type=jnp.float32)
        backward = backward + jnp.where(
            (slots < time_count - lag)[:, None, None],
            product[:time_count],
            jnp.zeros((), jnp.float32),
        )
        forward = forward + jnp.where(
            (slots >= time_count - lag - 1)[:, None, None], product[1:], jnp.zeros((), jnp.float32)
        )
        return (forward, backward)

    empty_rows = jnp.zeros((time_count, rows_each, states), jnp.float32)
    forward, backward = lax.fori_loop(0, time_count // 2, pair_step, (empty_rows, empty_rows))
    convolved = step_size * (forward + backward[::-1])
    row_ids = first_row + jnp.arange(rows_each, dtype=jnp.int32)
    row_rates = lax.dynamic_slice_in_dim(energies[0], first_row, rows_each, 0)
    decay_rows = jnp.exp(-step_size * row_rates)

    def advance(running, term):
        running = decay_rows[:, None] * running + term
        return (running, running)

    _, summed = lax.scan(advance, jnp.zeros((rows_each, states), jnp.float32), convolved)
    moments = jnp.arange(time_count).astype(jnp.float32) * step_size
    live_rows = row_ids < sector_sizes[0]
    free_part = jnp.where(
        live_rows[None, :],
        jnp.exp(-row_rates[None, :] * moments[:, None]),
        jnp.zeros((), jnp.float32),
    )
    diagonal = jnp.where(
        (row_ids[:, None] == positions[None, :])[None],
        free_part[:, :, None],
        jnp.zeros((), jnp.float32),
    )
    new_rows = (diagonal - step_size * summed).astype(jnp.bfloat16)
    return lax.all_to_all(new_rows, "tm", split_axis=0, concat_axis=1, tiled=True)[None]


MESH = pl.DeviceIdType.MESH
ROW_TILE = 16
LANES = 128
SUBLANES = 8
PARTS = 4


def flipped(index, mask):
    bit = 1
    while bit <= mask:
        if mask & bit:
            index = index + bit - 2 * bit * lax.rem(lax.div(index, bit), 2)
        bit *= 2
    return index


def last_hop(mask, part):
    bits = [1 << i for i in range(mask.bit_length()) if mask >> i & 1]
    if bits[0] == 1:
        return 1
    return bits[0] if part < PARTS // 2 else bits[-1]


def fused_kernel(
    times,
    sectors,
    size_ref,
    particle_ref,
    hole_ref,
    prop_ref,
    operator_ref,
    energy_ref,
    out_ref,
    history,
    lower_operator,
    turned,
    pair,
    up_rows,
    down_rows,
    below,
    above,
    energy_in,
    sums,
    fresh,
    strengths,
    operator_send,
    operator_recv,
    up_send,
    up_recv,
    down_send,
    down_recv,
    gather_send,
    gather_recv,
    strength_send,
    strength_recv,
    out_send,
    out_recv,
):
    states = prop_ref.shape[-1]
    rows = states // times
    half = states // 2
    piece_rows = states // PARTS
    step_size = 1.0 / times
    me = lax.axis_index("tm")
    sector = lax.axis_index("sector")
    has_below = sector > 0
    has_above = sector < sectors - 1

    barrier = pltpu.get_barrier_semaphore()
    for mask in range(1, times):
        pl.semaphore_signal(
            barrier, inc=1, device_id={"tm": flipped(me, mask)}, device_id_type=MESH
        )

    @pl.when(has_below)
    def _():
        pl.semaphore_signal(barrier, inc=1, device_id={"sector": sector - 1}, device_id_type=MESH)

    @pl.when(has_above)
    def _():
        pl.semaphore_signal(barrier, inc=1, device_id={"sector": sector + 1}, device_id_type=MESH)

    size = size_ref[0]
    live = (lax.broadcasted_iota(jnp.int32, (states, states), 0) < size) & (
        lax.broadcasted_iota(jnp.int32, (states, states), 1) < size
    )
    history[me] = jnp.where(
        live, prop_ref[0, 0].astype(jnp.float32), jnp.zeros((), jnp.float32)
    ).astype(jnp.bfloat16)
    first_line = lax.broadcasted_iota(jnp.int32, strengths.shape[1:], 0) == 0
    strengths[me] = jnp.where(first_line, particle_ref[0], hole_ref[0])

    neighbours = jnp.where(has_below, 1, 0) + jnp.where(has_above, 1, 0)
    pl.semaphore_wait(barrier, times - 1 + neighbours)

    def row_block(index):
        return pl.ds(pl.multiple_of(index * rows, rows), rows)

    def half_block(index):
        return pl.ds(pl.multiple_of(index * half, half), half)

    my_half = lax.rem(me, 2)

    def operator_copy():
        return pltpu.make_async_remote_copy(
            src_ref=operator_ref.at[0, half_block(my_half)],
            dst_ref=lower_operator.at[half_block(my_half)],
            send_sem=operator_send.at[0],
            recv_sem=operator_recv.at[0],
            device_id={"sector": sector + 1},
            device_id_type=MESH,
        )

    def share_copy(which):
        return pltpu.make_async_remote_copy(
            src_ref=lower_operator.at[half_block(which)],
            dst_ref=lower_operator.at[half_block(which)],
            send_sem=operator_send.at[1],
            recv_sem=operator_recv.at[1],
            device_id={"tm": flipped(me, 1)},
            device_id_type=MESH,
        )

    def up_copy(mask, step=1):
        block = row_block(flipped(me, mask))
        return pltpu.make_async_remote_copy(
            src_ref=up_rows.at[block],
            dst_ref=below.at[block],
            send_sem=up_send.at[mask],
            recv_sem=up_recv.at[mask],
            device_id={"sector": sector + step},
            device_id_type=MESH,
        )

    def down_copy(mask, step=-1):
        block = row_block(flipped(me, mask))
        return pltpu.make_async_remote_copy(
            src_ref=down_rows.at[block],
            dst_ref=above.at[block],
            send_sem=down_send.at[mask],
            recv_sem=down_recv.at[mask],
            device_id={"sector": sector + step},
            device_id_type=MESH,
        )

    def gather_copy(mask, part, block):
        piece = history.at[block, pl.ds(part * piece_rows, piece_rows)]
        return pltpu.make_async_remote_copy(
            src_ref=piece,
            dst_ref=piece,
            send_sem=gather_send.at[mask, part],
            recv_sem=gather_recv.at[mask, part],
            device_id={"tm": flipped(me, last_hop(mask, part))},
            device_id_type=MESH,
        )

    def strength_copy(mask, block):
        return pltpu.make_async_remote_copy(
            src_ref=strengths.at[block],
            dst_ref=strengths.at[block],
            send_sem=strength_send.at[mask],
            recv_sem=strength_recv.at[mask],
            device_id={"tm": flipped(me, mask)},
            device_id_type=MESH,
        )

    def gather_start(mask, part):
        gather_copy(mask, part, flipped(me, mask ^ last_hop(mask, part))).start()

    forward = list(range(PARTS))
    backward = forward[PARTS // 2 :] + forward[: PARTS // 2]
    mixed = [p for pair_of in zip(forward, backward) for p in pair_of][:PARTS]
    singles = [1 << i for i in range(1, times.bit_length() - 1)]
    order = {mask: (backward if i % 2 == 0 else forward) for i, mask in enumerate(singles)}
    started = {(mask, part) for mask in [1] + singles for part in range(PARTS)}
    arrived = set()
    for turn in range(PARTS):
        for mask in singles:
            gather_start(mask, order[mask][turn])
        gather_start(1, turn)

    @pl.when(has_above)
    def _():
        operator_copy().start()

    for mask in range(1, times):
        strength_copy(mask, me).start()

    def gather_arrive(mask, part):
        if (mask, part) in arrived:
            return
        arrived.add((mask, part))
        gather_copy(mask, part, flipped(me, mask)).wait_recv()
        for later in range(2, times):
            if (later, part) not in started and later ^ last_hop(later, part) == mask:
                started.add((later, part))
                gather_start(later, part)

    def send_up(mask, raised):
        up_rows[row_block(flipped(me, mask))] = lax.dot_general(
            raised, operator_ref[0], (((1,), (1,)), ((), ())), preferred_element_type=jnp.float32
        ).astype(jnp.bfloat16)

        @pl.when(has_above)
        def _():
            up_copy(mask).start()

    def send_down(mask, lowered):
        down_rows[row_block(flipped(me, mask))] = jnp.dot(
            lowered, lower_operator[...], preferred_element_type=jnp.float32
        ).astype(jnp.bfloat16)

        @pl.when(has_below)
        def _():
            down_copy(mask).start()

    def product_of(left, mask):
        return jnp.dot(
            left, history[flipped(me, mask)], preferred_element_type=jnp.float32
        ).astype(jnp.bfloat16)

    pair[0:rows] = operator_ref[0, row_block(me)]
    send_up(0, product_of(pair[0:rows], 0))
    for part in range(PARTS):
        gather_arrive(1, part)
    send_up(1, product_of(pair[0:rows], 1))
    for turn in range(PARTS // 2):
        for mask in singles:
            gather_arrive(mask, order[mask][turn])

    @pl.when(has_below)
    def _():
        pltpu.make_async_remote_copy(
            src_ref=lower_operator.at[half_block(my_half)],
            dst_ref=lower_operator.at[half_block(my_half)],
            send_sem=operator_send.at[0],
            recv_sem=operator_recv.at[0],
            device_id={"sector": sector - 1},
            device_id_type=MESH,
        ).wait_recv()
        share_copy(my_half).start()
        share_copy(1 - my_half).wait_recv()

    @pl.when(sector == 0)
    def _():
        lower_operator[...] = jnp.zeros_like(lower_operator)

    turned[...] = lower_operator[...].T
    pair[rows : 2 * rows] = turned[row_block(me)]
    for mask in range(2):
        send_down(mask, product_of(pair[rows : 2 * rows], mask))

    for turn in range(PARTS // 2, PARTS):
        for mask in singles:
            gather_arrive(mask, order[mask][turn])

    ranked = sorted(range(2, times), key=lambda m: (bin(m >> 1).count("1"), m & 1, m))
    for mask in ranked:
        for part in mixed:
            gather_arrive(mask, part)
        both = product_of(pair[...], mask)
        send_up(mask, both[0:rows])
        send_down(mask, both[rows : 2 * rows])

    @pl.when(sector == 0)
    def _():
        below[...] = jnp.zeros_like(below)

    @pl.when(sector == sectors - 1)
    def _():
        above[...] = jnp.zeros_like(above)

    row_ids = me * rows + lax.broadcasted_iota(jnp.int32, (rows, states), 0)
    column_ids = lax.broadcasted_iota(jnp.int32, (rows, states), 1)
    on_diagonal = row_ids == column_ids
    rates = jnp.sum(
        jnp.where(on_diagonal, energy_ref[...], jnp.zeros((), jnp.float32)), axis=1, keepdims=True
    )
    decay = jnp.exp(-step_size * rates)
    shown = on_diagonal & (row_ids < size)
    live_rows = (row_ids < size) & (column_ids < size)

    for mask in range(1, times):
        strength_copy(mask, flipped(me, mask)).wait_recv()

    @pl.when(has_below)
    def _():
        for mask in range(times):
            up_copy(mask, -1).wait_recv()

    @pl.when(has_above)
    def _():
        for mask in range(times):
            down_copy(mask, 1).wait_recv()

    for moment in range(times):
        place = pl.ds(moment * rows, rows)
        combined = strengths[moment, 0:1, 0:1] * below[place].astype(jnp.float32) + strengths[
            moment, 1:2, 0:1
        ] * above[place].astype(jnp.float32)
        energy_in[place] = jnp.where(live_rows, combined, jnp.zeros((), jnp.float32)).astype(
            jnp.bfloat16
        )

    def out_copy(moment, place):
        return pltpu.make_async_remote_copy(
            src_ref=fresh.at[moment],
            dst_ref=out_ref.at[0, 0, row_block(place)],
            send_sem=out_send.at[moment],
            recv_sem=out_recv.at[place],
            device_id={"tm": moment},
            device_id_type=MESH,
        )

    running = jnp.zeros((rows, states), jnp.float32)
    for moment in range(times):
        depth = (times - moment) * rows
        product = jnp.dot(
            energy_in[0:depth], history[moment], preferred_element_type=jnp.float32
        )
        if moment == 0:
            sums[...] = product
        else:
            sums[moment * rows : states] += product
        running = decay * running + step_size * sums[moment * rows : (moment + 1) * rows]
        free_part = jnp.where(
            shown, jnp.exp(-rates * (moment * step_size)), jnp.zeros((), jnp.float32)
        )
        fresh[moment] = (free_part - step_size * running).astype(jnp.bfloat16)

        @pl.when(me != moment)
        def _():
            out_copy(moment, me).start()

        @pl.when(me == moment)
        def _():
            out_ref[0, 0, row_block(me)] = fresh[moment]

    for mask in range(1, times):
        pltpu.make_async_remote_copy(
            src_ref=fresh.at[0],
            dst_ref=out_ref.at[0, 0, row_block(flipped(me, mask))],
            send_sem=out_send.at[0],
            recv_sem=out_recv.at[flipped(me, mask)],
            device_id={"tm": flipped(me, mask)},
            device_id_type=MESH,
        ).wait_recv()
    for moment in range(times):

        @pl.when(me != moment)
        def _():
            out_copy(moment, me).wait_send()

    for mask in range(1, times):
        strength_copy(mask, me).wait_send()
        for part in range(PARTS):
            gather_copy(mask, part, flipped(me, mask)).wait_send()

    @pl.when(has_below)
    def _():
        share_copy(my_half).wait_send()
        for mask in range(times):
            down_copy(mask).wait_send()

    @pl.when(has_above)
    def _():
        operator_copy().wait_send()
        for mask in range(times):
            up_copy(mask).wait_send()


def fused_device(propagator, rising_op, energies, hyb_particle, hyb_hole, sector_sizes):
    times = lax.axis_size("tm")
    states = propagator.shape[-1]
    square = (states, states)
    narrow, wide = jnp.bfloat16, jnp.float32
    vmem = pl.BlockSpec(memory_space=pltpu.VMEM)
    smem = pl.BlockSpec(memory_space=pltpu.SMEM)
    dma = pltpu.SemaphoreType.DMA
    return pl.pallas_call(
        functools.partial(fused_kernel, times, lax.axis_size("sector")),
        out_shape=jax.ShapeDtypeStruct(propagator.shape, narrow),
        in_specs=[smem, smem, smem, vmem, vmem, vmem],
        out_specs=vmem,
        scratch_shapes=[
            pltpu.VMEM((times,) + square, narrow),
            pltpu.VMEM(square, narrow),
            pltpu.VMEM(square, narrow),
            pltpu.VMEM((2 * (states // times), states), narrow),
            pltpu.VMEM(square, narrow),
            pltpu.VMEM(square, narrow),
            pltpu.VMEM(square, narrow),
            pltpu.VMEM(square, narrow),
            pltpu.VMEM(square, narrow),
            pltpu.VMEM(square, wide),
            pltpu.VMEM((times, states // times, states), narrow),
            pltpu.VMEM((times, SUBLANES, LANES), wide),
            dma((2,)),
            dma((2,)),
            dma((times,)),
            dma((times,)),
            dma((times,)),
            dma((times,)),
            dma((times, PARTS)),
            dma((times, PARTS)),
            dma((times,)),
            dma((times,)),
            dma((times,)),
            dma((times,)),
        ],
        compiler_params=pltpu.CompilerParams(
            collective_id=0, has_side_effects=True, vmem_limit_bytes=28 * 2**20
        ),
    )(sector_sizes, hyb_particle, hyb_hole, propagator, rising_op, energies)


def per_device(propagator, rising_op, energies, hyb_particle, hyb_hole, sector_sizes):
    times = lax.axis_size("tm")
    states = propagator.shape[-1]
    fits = (
        propagator.shape[1] == 1
        and times > 2
        and times & (times - 1) == 0
        and states % (times * ROW_TILE) == 0
        and states % (PARTS * ROW_TILE) == 0
        and states % LANES == 0
    )
    chosen = fused_device if fits else general_device
    return chosen(propagator, rising_op, energies, hyb_particle, hyb_hole, sector_sizes)


def solution(mesh):
    placed = (
        P("sector", "tm", None, None),
        P("sector", None, None),
        P("sector", None),
        P("tm"),
        P("tm"),
        P("sector"),
    )
    return jax.shard_map(
        per_device,
        mesh=mesh,
        in_specs=placed,
        out_specs=P("sector", "tm", None, None),
        check_vma=False,
    )
```

profile of v0, /device:TPU:15, one launch (start us, length us, event | category | flops | bytes accessed | tf_op | source)
XLA Modules:
  0.0 59.8 jit_solution(17631239105342948842)
XLA Ops:
  0.0 0.0 copy-start.2
  2.0 0.0 copy-done.2
  2.0 0.0 copy-start
  2.0 1.1 %copy-done = bf16[1,1,640,640]{3,2,1,0:T(8,128)(2,1)S(1)} copy-done((bf16[1,1,640,640]{3,2,1,0:T(8,128)(2,1)S(1)}, bf16[1,1,640,640]{3,2,1,0:T(8,128)(2,1)}, u32[]{:S(2)}) %copy-start) | copy-done | bytes 819224
  3.1 0.0 copy-start.1
  3.1 1.1 %copy-done.1 = bf16[1,640,640]{2,1,0:T(8,128)(2,1)S(1)} copy-done((bf16[1,640,640]{2,1,0:T(8,128)(2,1)S(1)}, bf16[1,640,640]{2,1,0:T(8,128)(2,1)}, u32[]{:S(2)}) %copy-start.1) | copy-done | bytes 819224
  4.3 54.7 %shard_map.64 = bf16[1,1,640,640]{3,2,1,0:T(8,128)(2,1)S(1)} custom-call(s32[1]{0:T(128)S(6)} %copy.10.size_ref, f32[1]{0:T(128)S(6)} %copy.8.particle_ref, f32[1]{0:T(128)S(6)} %copy.9.hole_ref, bf16[1,1,640,640]{3,2,1,0:T(8,128)(2,1)S(1)} %copy-done, bf16[1,640,640]{2,1,0:T(8,128)(2,1)S(1)} %copy-done.1, f32[1,640]{1,0:T(1,128)S(1)} %copy-done.2), custom_call_target="tpu_custom_call" | custom-call | tf_op jit(solution)/shard_map/pallas_call | solution.py:476
  59.0 0.9 %copy.11 = bf16[1,1,640,640]{3,2,1,0:T(8,128)(2,1)} copy(bf16[1,1,640,640]{3,2,1,0:T(8,128)(2,1)S(1)} %shard_map.64) | data formatting | bytes 1638400
Async XLA Ops:
  0.0 2.0 %copy-start.2 = (f32[1,640]{1,0:T(1,128)S(1)}, f32[1,640]{1,0:T(1,128)}, u32[]{:S(2)}) copy-start(f32[1,640]{1,0:T(1,128)} %energy_ref.1) | copy-start | bytes 7684
  2.0 1.1 %copy-start = (bf16[1,1,640,640]{3,2,1,0:T(8,128)(2,1)S(1)}, bf16[1,1,640,640]{3,2,1,0:T(8,128)(2,1)}, u32[]{:S(2)}) copy-start(bf16[1,1,640,640]{3,2,1,0:T(8,128)(2,1)} %prop_ref.1) | copy-start | bytes 2457604
  3.1 1.1 %copy-start.1 = (bf16[1,640,640]{2,1,0:T(8,128)(2,1)S(1)}, bf16[1,640,640]{2,1,0:T(8,128)(2,1)}, u32[]{:S(2)}) copy-start(bf16[1,640,640]{2,1,0:T(8,128)(2,1)} %operator_ref.1) | copy-start | bytes 2457604
where the time goes:
time: 60.1 us; the launch traced here: 59.8 us
  Pallas kernels  54.7 us (91%)
  local copies, waits for them, and re-layouts  3.18 us (5%)
  between operations  1.98 us (3%)
    pallas_call x1, Pallas kernels, fused_device(): pl.pallas_call(functools.partial(fused_kernel, times, lax.axis_size('sect...  54.7 us
    unnamed x7, local copies, waits for them, and re-layouts  3.18 us

commit v1 on v0

v1 whole, which is shorter than its diff:
```python
import functools
import jax
import jax.numpy as jnp
from jax import lax
from jax.experimental import pallas as pl
from jax.experimental.pallas import tpu as pltpu
from jax.sharding import PartitionSpec as P


def shifted(block, axis, distance):
    devices = range(lax.axis_size(axis))
    route = [(i - distance, i) for i in devices if i - distance in devices]
    return lax.ppermute(block, axis, route)


def general_device(propagator, rising_op, energies, hyb_particle, hyb_hole, sector_sizes):
    t_dev = propagator.shape[1]
    states = propagator.shape[2]
    time_count = t_dev * lax.axis_size("tm")
    step_size = 1.0 / time_count
    positions = jnp.arange(states, dtype=jnp.int32)
    live_mask = positions < sector_sizes[0]
    square = live_mask[:, None] & live_mask[None, :]
    masked_prop = jnp.where(square[None], propagator[0], jnp.zeros((), jnp.bfloat16))
    operator = rising_op[0]
    raised = jnp.einsum(
        "ik,tkl->til", operator, masked_prop, preferred_element_type=jnp.float32
    ).astype(jnp.bfloat16)
    upward = jnp.einsum("tik,jk->tij", raised, operator, preferred_element_type=jnp.float32).astype(
        jnp.bfloat16
    )
    from_below = shifted(upward, "sector", 1)
    from_above = shifted(masked_prop, "sector", -1)
    lowered = jnp.einsum(
        "ki,tkl->til", operator, from_above, preferred_element_type=jnp.float32
    ).astype(jnp.bfloat16)
    downward = jnp.einsum("tik,kl->til", lowered, operator, preferred_element_type=jnp.float32)
    combined = (
        hyb_particle[:, None, None] * from_below.astype(jnp.float32)
        + hyb_hole[:, None, None] * downward
    )
    self_energy = jnp.where(square[None], combined, jnp.zeros((), jnp.float32)).astype(jnp.bfloat16)
    rows_each = states // lax.axis_size("tm")
    first_row = lax.axis_index("tm") * rows_each
    lag_rows = lax.all_to_all(self_energy, "tm", split_axis=1, concat_axis=0, tiled=True)
    history = lax.all_gather(masked_prop, "tm", axis=0, tiled=True)
    mirrored = jnp.concatenate([history[::-1], history], 0)
    slots = jnp.arange(time_count, dtype=jnp.int32)
    wide_slots = jnp.arange(time_count + 1, dtype=jnp.int32)

    def pair_step(lag, sums):
        forward, backward = sums
        other = time_count - 1 - lag
        window = lax.dynamic_slice_in_dim(mirrored, lag, time_count + 1, 0)
        near = lax.dynamic_index_in_dim(lag_rows, lag, 0, keepdims=False)
        far = lax.dynamic_index_in_dim(lag_rows, other, 0, keepdims=False)
        left = jnp.where((wide_slots < time_count - lag)[:, None, None], near[None], far[None])
        product = jnp.einsum("uik,ukl->uil", left, window, preferred_element_type=jnp.float32)
        backward = backward + jnp.where(
            (slots < time_count - lag)[:, None, None],
            product[:time_count],
            jnp.zeros((), jnp.float32),
        )
        forward = forward + jnp.where(
            (slots >= time_count - lag - 1)[:, None, None], product[1:], jnp.zeros((), jnp.float32)
        )
        return (forward, backward)

    empty_rows = jnp.zeros((time_count, rows_each, states), jnp.float32)
    forward, backward = lax.fori_loop(0, time_count // 2, pair_step, (empty_rows, empty_rows))
    convolved = step_size * (forward + backward[::-1])
    row_ids = first_row + jnp.arange(rows_each, dtype=jnp.int32)
    row_rates = lax.dynamic_slice_in_dim(energies[0], first_row, rows_each, 0)
    decay_rows = jnp.exp(-step_size * row_rates)

    def advance(running, term):
        running = decay_rows[:, None] * running + term
        return (running, running)

    _, summed = lax.scan(advance, jnp.zeros((rows_each, states), jnp.float32), convolved)
    moments = jnp.arange(time_count).astype(jnp.float32) * step_size
    live_rows = row_ids < sector_sizes[0]
    free_part = jnp.where(
        live_rows[None, :],
        jnp.exp(-row_rates[None, :] * moments[:, None]),
        jnp.zeros((), jnp.float32),
    )
    diagonal = jnp.where(
        (row_ids[:, None] == positions[None, :])[None],
        free_part[:, :, None],
        jnp.zeros((), jnp.float32),
    )
    new_rows = (diagonal - step_size * summed).astype(jnp.bfloat16)
    return lax.all_to_all(new_rows, "tm", split_axis=0, concat_axis=1, tiled=True)[None]


MESH = pl.DeviceIdType.MESH
ROW_TILE = 16
LANES = 128
SUBLANES = 8
CORE, ACROSS, ALONG = 1, 2, 4
PIECES = 4
VMEM_GRANT = 211 * 2**18


def flipped(index, mask):
    bit = 1
    while bit <= mask:
        if mask & bit:
            index = index + bit - 2 * bit * lax.rem(lax.div(index, bit), 2)
        bit *= 2
    return index


def fused_kernel(
    times,
    sectors,
    size_hbm,
    particle_hbm,
    hole_hbm,
    prop_hbm,
    operator_hbm,
    energy_hbm,
    out_ref,
    size_ref,
    particle_ref,
    hole_ref,
    energy_ref,
    history,
    operator,
    raiser,
    turned,
    turned_in,
    pair,
    up_rows,
    down_rows,
    below,
    above,
    energy_in,
    sums,
    running,
    fresh,
    passing,
    strengths,
    load_sem,
    turned_send,
    turned_recv,
    up_send,
    up_recv,
    down_send,
    down_recv,
    piece_send,
    piece_recv,
    strength_send,
    strength_recv,
    out_send,
    out_recv,
    passing_send,
    passing_recv,
):
    states = prop_hbm.shape[-1]
    rows = states // times
    quarter = states // PIECES
    step_size = 1.0 / times
    me = lax.axis_index("tm")
    sector = lax.axis_index("sector")
    has_below = sector > 0
    has_above = sector < sectors - 1
    core = lax.rem(me, 2)
    even = me - core
    partner = flipped(me, CORE)
    x_even, y_even = flipped(even, ACROSS), flipped(even, ALONG)
    d_even = flipped(even, ACROSS | ALONG)

    loads = [
        pltpu.make_async_copy(src, dst, load_sem.at[i])
        for i, (src, dst) in enumerate(
            [
                (prop_hbm.at[0, 0], history.at[me]),
                (size_hbm, size_ref),
                (operator_hbm.at[0], operator),
                (particle_hbm, particle_ref),
                (hole_hbm, hole_ref),
                (energy_hbm, energy_ref),
            ]
        )
    ]
    barrier = pltpu.get_barrier_semaphore()
    for mask in range(1, times):
        pl.semaphore_signal(
            barrier, inc=1, device_id={"tm": flipped(me, mask)}, device_id_type=MESH
        )

    @pl.when(has_below)
    def _():
        pl.semaphore_signal(barrier, inc=1, device_id={"sector": sector - 1}, device_id_type=MESH)

    @pl.when(has_above)
    def _():
        pl.semaphore_signal(barrier, inc=1, device_id={"sector": sector + 1}, device_id_type=MESH)

    for load in loads:
        load.start()

    def row_block(index):
        return pl.ds(pl.multiple_of(index * rows, rows), rows)

    def piece_copy(step, time, q):
        piece = history.at[time, pl.ds(pl.multiple_of(q * quarter, quarter), quarter)]
        return pltpu.make_async_remote_copy(
            src_ref=piece,
            dst_ref=piece,
            send_sem=piece_send.at[step.bit_length() - 1, time, q],
            recv_sem=piece_recv.at[time, q],
            device_id={"tm": flipped(me, step)},
            device_id_type=MESH,
        )

    mine = [2 * core, 2 * core + 1]
    other = [2 - 2 * core, 3 - 2 * core]

    def turned_copy(step=1):
        return pltpu.make_async_remote_copy(
            src_ref=turned,
            dst_ref=turned_in,
            send_sem=turned_send,
            recv_sem=turned_recv,
            device_id={"sector": sector + step},
            device_id_type=MESH,
        )

    def up_copy(slot, time, step=1):
        block = row_block(time)
        return pltpu.make_async_remote_copy(
            src_ref=up_rows.at[block],
            dst_ref=below.at[block],
            send_sem=up_send.at[slot],
            recv_sem=up_recv.at[slot],
            device_id={"sector": sector + step},
            device_id_type=MESH,
        )

    def down_copy(slot, time, step=-1):
        block = row_block(time)
        return pltpu.make_async_remote_copy(
            src_ref=down_rows.at[block],
            dst_ref=above.at[block],
            send_sem=down_send.at[slot],
            recv_sem=down_recv.at[slot],
            device_id={"sector": sector + step},
            device_id_type=MESH,
        )

    def strength_copy(mask, block):
        return pltpu.make_async_remote_copy(
            src_ref=strengths.at[block],
            dst_ref=strengths.at[block],
            send_sem=strength_send.at[mask],
            recv_sem=strength_recv.at[mask],
            device_id={"tm": flipped(me, mask)},
            device_id_type=MESH,
        )

    def out_copy(moment, place):
        return pltpu.make_async_remote_copy(
            src_ref=fresh.at[moment],
            dst_ref=out_ref.at[0, 0, row_block(place)],
            send_sem=out_send.at[moment],
            recv_sem=out_recv.at[place],
            device_id={"tm": moment},
            device_id_type=MESH,
        )

    def passing_copy():
        return pltpu.make_async_remote_copy(
            src_ref=fresh.at[d_even],
            dst_ref=passing,
            send_sem=passing_send.at[0],
            recv_sem=passing_recv,
            device_id={"tm": flipped(me, ALONG)},
            device_id_type=MESH,
        )

    def passed_copy():
        return pltpu.make_async_remote_copy(
            src_ref=passing,
            dst_ref=out_ref.at[0, 0, row_block(flipped(me, ALONG))],
            send_sem=passing_send.at[1],
            recv_sem=out_recv.at[flipped(me, ALONG)],
            device_id={"tm": x_even},
            device_id_type=MESH,
        )

    loads[0].wait()
    for load in loads[3:]:
        load.wait()
    first_line = lax.broadcasted_iota(jnp.int32, strengths.shape[1:], 0) == 0
    strengths[me] = jnp.where(first_line, particle_ref[0], hole_ref[0])
    neighbours = jnp.where(has_below, 1, 0) + jnp.where(has_above, 1, 0)
    pl.semaphore_wait(barrier, times - 1 + neighbours)

    def links_start(time):
        for step, r in ((ACROSS, 0), (ALONG, 1), (ACROSS, 1), (ALONG, 0)):
            piece_copy(step, time, mine[r]).start()

    for mask in range(1, times):
        strength_copy(mask, me).start()
    for q in other:
        piece_copy(CORE, me, q).start()

    @pl.when(core == 0)
    def _():
        links_start(me)

    for q in mine:
        piece_copy(CORE, me, q).start()
    loads[2].wait()
    row_ids = me * rows + lax.broadcasted_iota(jnp.int32, (rows, states), 0)
    column_ids = lax.broadcasted_iota(jnp.int32, (rows, states), 1)
    on_diagonal = row_ids == column_ids
    chosen = jnp.where(on_diagonal, 1.0, 0.0).astype(jnp.bfloat16)
    turned[...] = lax.dot_general(
        chosen, operator[...], (((1,), (1,)), ((), ())), preferred_element_type=jnp.float32
    ).astype(jnp.bfloat16)

    @pl.when(has_above)
    def _():
        turned_copy().start()

    loads[1].wait()
    size = size_ref[0]
    live_columns = lax.broadcasted_iota(jnp.int32, (states, states), 1) < size
    live_line = column_ids < size
    raiser[...] = jnp.where(live_columns, operator[...].astype(jnp.float32), 0.0).astype(
        jnp.bfloat16
    )
    for q in mine:
        piece_copy(CORE, partner, q).wait_recv()

    links_start(partner)

    @pl.when(core == 1)
    def _():
        links_start(me)

    def product_of(left, time):
        return jnp.dot(left, history[time], preferred_element_type=jnp.float32)

    def send_up(slot, time, raised):
        up_rows[row_block(time)] = lax.dot_general(
            raised.astype(jnp.bfloat16),
            raiser[...],
            (((1,), (1,)), ((), ())),
            preferred_element_type=jnp.float32,
        ).astype(jnp.bfloat16)

        @pl.when(has_above)
        def _():
            up_copy(slot, time).start()

    def send_down(slot, time, lowered):
        down_rows[row_block(time)] = jnp.where(live_line, lowered, 0.0).astype(jnp.bfloat16)

        @pl.when(has_below)
        def _():
            down_copy(slot, time).start()

    def arrive(step, time, r):
        piece_copy(step, time, mine[r]).wait_recv()
        piece_copy(CORE, time, mine[r]).start()

    def relay(step, time, r):
        piece_copy(step, time, mine[r]).start()

    def shared(time):
        for q in other:
            piece_copy(CORE, time, q).wait_recv()

    order = [me, partner, x_even, y_even, x_even + 1, y_even + 1, d_even, d_even + 1]
    last = order[-1]

    pair[0:rows] = raiser[row_block(me)]
    send_up(0, me, product_of(pair[0:rows], me))
    shared(partner)
    send_up(1, partner, product_of(pair[0:rows], partner))

    rates = jnp.sum(
        jnp.where(on_diagonal, energy_ref[...], jnp.zeros((), jnp.float32)), axis=1, keepdims=True
    )
    decay = jnp.exp(-step_size * rates)
    running[...] = jnp.zeros_like(running)
    sums[...] = jnp.zeros_like(sums)

    @pl.when(jnp.logical_not(has_below))
    def _():
        turned_in[...] = jnp.zeros_like(turned_in)
        below[...] = jnp.zeros_like(below)

    @pl.when(jnp.logical_not(has_above))
    def _():
        above[...] = jnp.zeros_like(above)

    arrive(ACROSS, x_even, 0)
    relay(ALONG, x_even, 0)
    arrive(ALONG, y_even, 1)
    relay(ACROSS, y_even, 1)

    @pl.when(has_below)
    def _():
        turned_copy(-1).wait_recv()

    pair[rows : 2 * rows] = jnp.where(
        live_line, turned_in[...].astype(jnp.float32), 0.0
    ).astype(jnp.bfloat16)
    for slot in range(2):
        send_down(slot, order[slot], product_of(pair[rows : 2 * rows], order[slot]))

    arrive(ACROSS, x_even, 1)
    arrive(ALONG, y_even, 0)

    def both(slot):
        time = order[slot]
        shared(time)
        result = product_of(pair[...], time)
        send_down(slot, time, result[rows : 2 * rows])
        send_up(slot, time, result[0:rows])

    live_rows = (row_ids < size) & (column_ids < size)
    shown = on_diagonal & (row_ids < size)

    def combine(*slots):
        places = [row_block(order[slot]) for slot in slots]

        @pl.when(has_below)
        def _():
            for slot in slots:
                up_copy(slot, order[slot], -1).wait_recv()

        @pl.when(has_above)
        def _():
            for slot in slots:
                down_copy(slot, order[slot], 1).wait_recv()

        lowered = jnp.concatenate([above[place] for place in places], 0)
        downward = jnp.dot(lowered, operator[...], preferred_element_type=jnp.float32)
        for i, (slot, place) in enumerate(zip(slots, places)):
            level = strengths[order[slot]]
            combined = (
                level[0:1, 0:1] * below[place].astype(jnp.float32)
                + level[1:2, 0:1] * downward[i * rows : (i + 1) * rows]
            )
            energy_in[place] = jnp.where(live_rows, combined, jnp.zeros((), jnp.float32)).astype(
                jnp.bfloat16
            )

    def convolve(lag_even, *times_in):
        for time in times_in:

            @pl.when(lag_even + time < times)
            def _():
                left = energy_in[pl.ds(pl.multiple_of(lag_even * rows, rows), 2 * rows)]
                first = pl.multiple_of((lag_even + time) * rows, rows)
                sums[pl.ds(first, 2 * rows)] += jnp.dot(
                    left, history[time], preferred_element_type=jnp.float32
                )

    def finish(moment):
        place = row_block(moment)
        value = decay * running[...] + step_size * sums[place]
        running[...] = value
        instant = jnp.asarray(moment, jnp.int32).astype(jnp.float32) * step_size
        free_part = jnp.where(shown, jnp.exp(-rates * instant), jnp.zeros((), jnp.float32))
        fresh[moment] = jnp.where(
            live_rows, free_part - step_size * value, jnp.zeros((), jnp.float32)
        ).astype(jnp.bfloat16)

        @pl.when((me != moment) & (d_even != moment))
        def _():
            out_copy(moment, me).start()

        @pl.when(d_even == moment)
        def _():
            passing_copy().start()

        @pl.when(me == moment)
        def _():
            out_ref[0, 0, row_block(me)] = fresh[moment]

    x_odd, y_odd = x_even + 1, y_even + 1
    for mask in range(1, times):
        strength_copy(mask, flipped(me, mask)).wait_recv()
    both(2)
    both(3)
    combine(0, 1)
    convolve(even, even, even + 1)
    arrive(ACROSS, x_odd, 0)
    relay(ALONG, x_odd, 0)
    arrive(ALONG, y_odd, 1)
    relay(ACROSS, y_odd, 1)
    convolve(even, x_even, y_even)
    arrive(ACROSS, x_odd, 1)
    arrive(ALONG, y_odd, 0)
    combine(2, 3)
    both(4)
    both(5)
    arrive(ALONG, d_even, 0)
    arrive(ACROSS, d_even, 1)
    convolve(even, x_odd, y_odd)
    both(6)
    convolve(even, d_even)
    arrive(ALONG, last, 0)
    arrive(ACROSS, last, 1)
    combine(4, 5)
    convolve(x_even, y_even, y_odd)
    both(7)
    convolve(y_even, x_even, x_odd)
    convolve(x_even, even, even + 1, x_even, x_odd)
    convolve(y_even, even, even + 1, y_even, y_odd)
    for moment in range(times):

        @pl.when(moment < d_even)
        def _():
            finish(moment)

    convolve(even, last)
    convolve(x_even, d_even, last)
    convolve(y_even, d_even, last)
    combine(6, 7)
    for moment in range(times):
        convolve(d_even, moment)

        @pl.when(d_even + moment < times)
        def _():
            finish(d_even + moment)

    passing_copy().wait_recv()
    passed_copy().start()
    for mask in range(1, times):
        pltpu.make_async_remote_copy(
            src_ref=fresh.at[0],
            dst_ref=out_ref.at[0, 0, row_block(flipped(me, mask))],
            send_sem=out_send.at[0],
            recv_sem=out_recv.at[flipped(me, mask)],
            device_id={"tm": flipped(me, mask)},
            device_id_type=MESH,
        ).wait_recv()
    for moment in range(times):

        @pl.when((me != moment) & (d_even != moment))
        def _():
            out_copy(moment, me).wait_send()

    passing_copy().wait_send()
    passed_copy().wait_send()
    for mask in range(1, times):
        strength_copy(mask, me).wait_send()
    for q in mine + other:
        piece_copy(CORE, me, q).wait_send()
    for time in (even, even + 1):
        for step in (ACROSS, ALONG):
            for q in mine:
                piece_copy(step, time, q).wait_send()
    for parity in range(2):
        for base in (x_even, y_even, d_even):
            for q in mine:
                piece_copy(CORE, base + parity, q).wait_send()
        piece_copy(ALONG, x_even + parity, mine[0]).wait_send()
        piece_copy(ACROSS, y_even + parity, mine[1]).wait_send()

    @pl.when(has_below)
    def _():
        for slot in range(times):
            down_copy(slot, order[slot]).wait_send()

    @pl.when(has_above)
    def _():
        turned_copy().wait_send()
        for slot in range(times):
            up_copy(slot, order[slot]).wait_send()


def fused_device(propagator, rising_op, energies, hyb_particle, hyb_hole, sector_sizes):
    times = lax.axis_size("tm")
    states = propagator.shape[-1]
    rows = states // times
    square = (states, states)
    narrow, wide = jnp.bfloat16, jnp.float32
    anywhere = pl.BlockSpec(memory_space=pltpu.HBM)
    dma = pltpu.SemaphoreType.DMA
    return pl.pallas_call(
        functools.partial(fused_kernel, times, lax.axis_size("sector")),
        out_shape=jax.ShapeDtypeStruct(propagator.shape, narrow),
        in_specs=[anywhere] * 6,
        out_specs=pl.BlockSpec(memory_space=pltpu.VMEM),
        scratch_shapes=[
            pltpu.SMEM((1,), jnp.int32),
            pltpu.SMEM((1,), wide),
            pltpu.SMEM((1,), wide),
            pltpu.VMEM(energies.shape, wide),
            pltpu.VMEM((times,) + square, narrow),
            pltpu.VMEM(square, narrow),
            pltpu.VMEM(square, narrow),
            pltpu.VMEM((rows, states), narrow),
            pltpu.VMEM((rows, states), narrow),
            pltpu.VMEM((2 * rows, states), narrow),
            pltpu.VMEM(square, narrow),
            pltpu.VMEM(square, narrow),
            pltpu.VMEM(square, narrow),
            pltpu.VMEM(square, narrow),
            pltpu.VMEM(square, narrow),
            pltpu.VMEM((states + rows, states), wide),
            pltpu.VMEM((rows, states), wide),
            pltpu.VMEM((times, rows, states), narrow),
            pltpu.VMEM((rows, states), narrow),
            pltpu.VMEM((times, SUBLANES, LANES), wide),
            dma((6,)),
            dma,
            dma,
            dma((times,)),
            dma((times,)),
            dma((times,)),
            dma((times,)),
            dma((3, times, PIECES)),
            dma((times, PIECES)),
            dma((times,)),
            dma((times,)),
            dma((times,)),
            dma((times,)),
            dma((2,)),
            dma,
        ],
        compiler_params=pltpu.CompilerParams(
            collective_id=0, has_side_effects=True, vmem_limit_bytes=VMEM_GRANT
        ),
    )(sector_sizes, hyb_particle, hyb_hole, propagator, rising_op, energies)


def per_device(propagator, rising_op, energies, hyb_particle, hyb_hole, sector_sizes):
    times = lax.axis_size("tm")
    states = propagator.shape[-1]
    fits = (
        propagator.shape[1] == 1
        and times == (CORE | ACROSS | ALONG) + 1
        and states % (times * ROW_TILE) == 0
        and states % (PIECES * ROW_TILE) == 0
        and states % LANES == 0
    )
    chosen = fused_device if fits else general_device
    return chosen(propagator, rising_op, energies, hyb_particle, hyb_hole, sector_sizes)


def solution(mesh):
    placed = (
        P("sector", "tm", None, None),
        P("sector", None, None),
        P("sector", None),
        P("tm"),
        P("tm"),
        P("sector"),
    )
    return jax.shard_map(
        per_device,
        mesh=mesh,
        in_specs=placed,
        out_specs=P("sector", "tm", None, None),
        check_vma=False,
    )
```

time: 60.1 us -> 55.3 us (0.920)
  the two profiles are of different devices: /device:TPU:15 before, /device:TPU:0 now
where the time goes in v1:
time: 55.3 us; the launch traced here: 55.1 us
  Pallas kernels  52.2 us (94%)
  between operations  1.97 us (4%)
  local copies, waits for them, and re-layouts  0.9 us (2%)
    pallas_call x1, Pallas kernels, fused_device(): pl.pallas_call(functools.partial(fused_kernel, times, lax.axis_size('sect...  52.2 us

profile of v1, /device:TPU:0, one launch (start us, length us, event | category | flops | bytes accessed | tf_op | source)
XLA Modules:
  0.0 55.1 jit_solution(10963397134957038291)
XLA Ops:
  0.0 0.0 copy-start
  2.0 0.0 copy-done
  2.0 52.2 %shard_map.64 = bf16[1,1,640,640]{3,2,1,0:T(8,128)(2,1)S(1)} custom-call(s32[1]{0:T(128)S(6)} %copy.10.size_hbm, f32[1]{0:T(128)S(6)} %copy.8.particle_hbm, f32[1]{0:T(128)S(6)} %copy.9.hole_hbm, bf16[1,1,640,640]{3,2,1,0:T(8,128)(2,1)} %prop_hbm.1, bf16[1,640,640]{2,1,0:T(8,128)(2,1)} %operator_hbm.1, f32[1,640]{1,0:T(1,128)S(1)} %copy-done), custom_call_target="tpu_custom_call" | custom-call | tf_op jit(solution)/shard_map/pallas_call | solution.py:590
  54.2 0.9 %copy.11 = bf16[1,1,640,640]{3,2,1,0:T(8,128)(2,1)} copy(bf16[1,1,640,640]{3,2,1,0:T(8,128)(2,1)S(1)} %shard_map.64) | data formatting | bytes 1638400
Async XLA Ops:
  0.0 2.0 %copy-start = (f32[1,640]{1,0:T(1,128)S(1)}, f32[1,640]{1,0:T(1,128)}, u32[]{:S(2)}) copy-start(f32[1,640]{1,0:T(1,128)} %energy_hbm.1) | copy-start | bytes 7684

commit v2 on v1

--- a/solution.py
+++ b/solution.py
@@ -129,6 +129,7 @@
     history,
     operator,
     raiser,
+    raiser_turned,
     turned,
     turned_in,
     pair,
@@ -140,7 +141,6 @@
     sums,
     running,
     fresh,
-    passing,
     strengths,
     load_sem,
     turned_send,
@@ -155,8 +155,6 @@
     strength_recv,
     out_send,
     out_recv,
-    passing_send,
-    passing_recv,
 ):
     states = prop_hbm.shape[-1]
     rows = states // times
@@ -271,26 +269,6 @@
             device_id_type=MESH,
         )
 
-    def passing_copy():
-        return pltpu.make_async_remote_copy(
-            src_ref=fresh.at[d_even],
-            dst_ref=passing,
-            send_sem=passing_send.at[0],
-            recv_sem=passing_recv,
-            device_id={"tm": flipped(me, ALONG)},
-            device_id_type=MESH,
-        )
-
-    def passed_copy():
-        return pltpu.make_async_remote_copy(
-            src_ref=passing,
-            dst_ref=out_ref.at[0, 0, row_block(flipped(me, ALONG))],
-            send_sem=passing_send.at[1],
-            recv_sem=out_recv.at[flipped(me, ALONG)],
-            device_id={"tm": x_even},
-            device_id_type=MESH,
-        )
-
     loads[0].wait()
     for load in loads[3:]:
         load.wait()
@@ -347,11 +325,8 @@
         return jnp.dot(left, history[time], preferred_element_type=jnp.float32)
 
     def send_up(slot, time, raised):
-        up_rows[row_block(time)] = lax.dot_general(
-            raised.astype(jnp.bfloat16),
-            raiser[...],
-            (((1,), (1,)), ((), ())),
-            preferred_element_type=jnp.float32,
+        up_rows[row_block(time)] = jnp.dot(
+            raised.astype(jnp.bfloat16), raiser_turned[...], preferred_element_type=jnp.float32
         ).astype(jnp.bfloat16)
 
         @pl.when(has_above)
@@ -380,6 +355,7 @@
     last = order[-1]
 
     pair[0:rows] = raiser[row_block(me)]
+    raiser_turned[...] = raiser[...].T
     send_up(0, me, product_of(pair[0:rows], me))
     shared(partner)
     send_up(1, partner, product_of(pair[0:rows], partner))
@@ -453,16 +429,18 @@
                 jnp.bfloat16
             )
 
-    def convolve(lag_even, *times_in):
-        for time in times_in:
-
-            @pl.when(lag_even + time < times)
-            def _():
-                left = energy_in[pl.ds(pl.multiple_of(lag_even * rows, rows), 2 * rows)]
-                first = pl.multiple_of((lag_even + time) * rows, rows)
-                sums[pl.ds(first, 2 * rows)] += jnp.dot(
-                    left, history[time], preferred_element_type=jnp.float32
-                )
+    def accumulate(lag_even, *bases):
+        left = energy_in[pl.ds(pl.multiple_of(lag_even * rows, rows), 2 * rows)]
+        for base in bases:
+            first = pl.multiple_of((lag_even + base) * rows, rows)
+            sums[pl.ds(first, 2 * rows)] += jnp.dot(
+                left, history[base], preferred_element_type=jnp.float32
+            )
+
+    def convolve(lag_even, *bases):
+        @pl.when(lag_even + bases[0] < times)
+        def _():
+            accumulate(lag_even, *bases)
 
     def finish(moment):
         place = row_block(moment)
@@ -474,13 +452,9 @@
             live_rows, free_part - step_size * value, jnp.zeros((), jnp.float32)
         ).astype(jnp.bfloat16)
 
-        @pl.when((me != moment) & (d_even != moment))
+        @pl.when((me != moment))
         def _():
             out_copy(moment, me).start()
-
-        @pl.when(d_even == moment)
-        def _():
-            passing_copy().start()
 
         @pl.when(me == moment)
         def _():
@@ -497,7 +471,8 @@
     relay(ALONG, x_odd, 0)
     arrive(ALONG, y_odd, 1)
     relay(ACROSS, y_odd, 1)
-    convolve(even, x_even, y_even)
+    convolve(even, x_even)
+    convolve(even, y_even)
     arrive(ACROSS, x_odd, 1)
     arrive(ALONG, y_odd, 0)
     combine(2, 3)
@@ -505,36 +480,51 @@
     both(5)
     arrive(ALONG, d_even, 0)
     arrive(ACROSS, d_even, 1)
-    convolve(even, x_odd, y_odd)
+    convolve(even, x_odd)
+    convolve(even, y_odd)
     both(6)
-    convolve(even, d_even)
+    accumulate(even, d_even)
     arrive(ALONG, last, 0)
     arrive(ACROSS, last, 1)
     combine(4, 5)
-    convolve(x_even, y_even, y_odd)
+
+    def finish_between(start, stop, allowed):
+        for moment in range(start, stop, 2):
+
+            @pl.when(allowed & (moment < d_even))
+            def _():
+                finish(moment)
+                finish(moment + 1)
+
+    first_half = d_even >= times // 2
+    convolve(x_even, even, even + 1)
+    convolve(x_even, x_even, x_odd)
+    finish_between(0, times // 2, first_half)
+    convolve(y_even, y_even, y_odd)
+    finish_between(0, times // 2, jnp.logical_not(first_half))
     both(7)
-    convolve(y_even, x_even, x_odd)
-    convolve(x_even, even, even + 1, x_even, x_odd)
-    convolve(y_even, even, even + 1, y_even, y_odd)
-    for moment in range(times):
-
-        @pl.when(moment < d_even)
-        def _():
-            finish(moment)
-
-    convolve(even, last)
+    accumulate(x_even, y_even, y_odd)
+    accumulate(y_even, x_even, x_odd)
+    convolve(y_even, even, even + 1)
+    finish_between(times // 2, times, first_half)
+    accumulate(even, last)
     convolve(x_even, d_even, last)
     convolve(y_even, d_even, last)
-    combine(6, 7)
-    for moment in range(times):
-        convolve(d_even, moment)
+    combine(6)
+    sums[row_block(d_even)] += jnp.dot(
+        energy_in[row_block(d_even)], history[0], preferred_element_type=jnp.float32
+    )
+    finish(d_even)
+    combine(7)
+    for moment in range(0, times, 2):
 
         @pl.when(d_even + moment < times)
         def _():
-            finish(d_even + moment)
-
-    passing_copy().wait_recv()
-    passed_copy().start()
+            accumulate(d_even, moment, moment + 1)
+            if moment > 0:
+                finish(d_even + moment)
+            finish(d_even + moment + 1)
+
     for mask in range(1, times):
         pltpu.make_async_remote_copy(
             src_ref=fresh.at[0],
@@ -546,12 +536,10 @@
         ).wait_recv()
     for moment in range(times):
 
-        @pl.when((me != moment) & (d_even != moment))
+        @pl.when((me != moment))
         def _():
             out_copy(moment, me).wait_send()
 
-    passing_copy().wait_send()
-    passed_copy().wait_send()
     for mask in range(1, times):
         strength_copy(mask, me).wait_send()
     for q in mine + other:
@@ -600,6 +588,7 @@
             pltpu.VMEM((times,) + square, narrow),
             pltpu.VMEM(square, narrow),
             pltpu.VMEM(square, narrow),
+            pltpu.VMEM(square, narrow),
             pltpu.VMEM((rows, states), narrow),
             pltpu.VMEM((rows, states), narrow),
             pltpu.VMEM((2 * rows, states), narrow),
@@ -611,7 +600,6 @@
             pltpu.VMEM((states + rows, states), wide),
             pltpu.VMEM((rows, states), wide),
             pltpu.VMEM((times, rows, states), narrow),
-            pltpu.VMEM((rows, states), narrow),
             pltpu.VMEM((times, SUBLANES, LANES), wide),
             dma((6,)),
             dma,
@@ -626,8 +614,6 @@
             dma((times,)),
             dma((times,)),
             dma((times,)),
-            dma((2,)),
-            dma,
         ],
         compiler_params=pltpu.CompilerParams(
             collective_id=0, has_side_effects=True, vmem_limit_bytes=VMEM_GRANT

time: 55.3 us -> 52.4 us (0.948)
  the two profiles are of different devices: /device:TPU:0 before, /device:TPU:15 now
where the time goes in v2:
time: 52.4 us; the launch traced here: 52.2 us
  Pallas kernels  49.4 us (94%)
  between operations  1.97 us (4%)
  local copies, waits for them, and re-layouts  0.9 us (2%)
    pallas_call x1, Pallas kernels, fused_device(): pl.pallas_call(functools.partial(fused_kernel, times, lax.axis_size('sect...  49.4 us

profile of v2, /device:TPU:15, one launch (start us, length us, event | category | flops | bytes accessed | tf_op | source)
XLA Modules:
  0.0 52.2 jit_solution(14448109934061022401)
XLA Ops:
  0.0 0.0 copy-start
  2.0 0.0 copy-done
  2.0 49.4 %shard_map.64 = bf16[1,1,640,640]{3,2,1,0:T(8,128)(2,1)S(1)} custom-call(s32[1]{0:T(128)S(6)} %copy.10.size_hbm, f32[1]{0:T(128)S(6)} %copy.8.particle_hbm, f32[1]{0:T(128)S(6)} %copy.9.hole_hbm, bf16[1,1,640,640]{3,2,1,0:T(8,128)(2,1)} %prop_hbm.1, bf16[1,640,640]{2,1,0:T(8,128)(2,1)} %operator_hbm.1, f32[1,640]{1,0:T(1,128)S(1)} %copy-done), custom_call_target="tpu_custom_call" | custom-call | tf_op jit(solution)/shard_map/pallas_call | solution.py:578
  51.3 0.9 %copy.11 = bf16[1,1,640,640]{3,2,1,0:T(8,128)(2,1)} copy(bf16[1,1,640,640]{3,2,1,0:T(8,128)(2,1)S(1)} %shard_map.64) | data formatting | bytes 1638400
Async XLA Ops:
  0.0 2.0 %copy-start = (f32[1,640]{1,0:T(1,128)S(1)}, f32[1,640]{1,0:T(1,128)}, u32[]{:S(2)}) copy-start(f32[1,640]{1,0:T(1,128)} %energy_hbm.1) | copy-start | bytes 7684

commit v3 on v2

--- a/solution.py
+++ b/solution.py
@@ -203,13 +203,13 @@
     def row_block(index):
         return pl.ds(pl.multiple_of(index * rows, rows), rows)
 
-    def piece_copy(step, time, q):
+    def piece_copy(step, time, q, kind):
         piece = history.at[time, pl.ds(pl.multiple_of(q * quarter, quarter), quarter)]
         return pltpu.make_async_remote_copy(
             src_ref=piece,
             dst_ref=piece,
-            send_sem=piece_send.at[step.bit_length() - 1, time, q],
-            recv_sem=piece_recv.at[time, q],
+            send_sem=piece_send,
+            recv_sem=piece_recv.at[time, kind],
             device_id={"tm": flipped(me, step)},
             device_id_type=MESH,
         )
@@ -227,13 +227,16 @@
             device_id_type=MESH,
         )
 
+    def signal_of(slot):
+        return slot // 2 if slot < times - 2 else slot - times // 2 + 1
+
     def up_copy(slot, time, step=1):
         block = row_block(time)
         return pltpu.make_async_remote_copy(
             src_ref=up_rows.at[block],
             dst_ref=below.at[block],
-            send_sem=up_send.at[slot],
-            recv_sem=up_recv.at[slot],
+            send_sem=up_send,
+            recv_sem=up_recv.at[signal_of(slot)],
             device_id={"sector": sector + step},
             device_id_type=MESH,
         )
@@ -243,18 +246,18 @@
         return pltpu.make_async_remote_copy(
             src_ref=down_rows.at[block],
             dst_ref=above.at[block],
-            send_sem=down_send.at[slot],
-            recv_sem=down_recv.at[slot],
+            send_sem=down_send,
+            recv_sem=down_recv.at[signal_of(slot)],
             device_id={"sector": sector + step},
             device_id_type=MESH,
         )
 
-    def strength_copy(mask, block):
+    def strength_copy(mask, block, count=1):
         return pltpu.make_async_remote_copy(
-            src_ref=strengths.at[block],
-            dst_ref=strengths.at[block],
-            send_sem=strength_send.at[mask],
-            recv_sem=strength_recv.at[mask],
+            src_ref=strengths.at[pl.ds(block, count)],
+            dst_ref=strengths.at[pl.ds(block, count)],
+            send_sem=strength_send,
+            recv_sem=strength_recv,
             device_id={"tm": flipped(me, mask)},
             device_id_type=MESH,
         )
@@ -263,8 +266,8 @@
         return pltpu.make_async_remote_copy(
             src_ref=fresh.at[moment],
             dst_ref=out_ref.at[0, 0, row_block(place)],
-            send_sem=out_send.at[moment],
-            recv_sem=out_recv.at[place],
+            send_sem=out_send,
+            recv_sem=out_recv,
             device_id={"tm": moment},
             device_id_type=MESH,
         )
@@ -279,19 +282,22 @@
 
     def links_start(time):
         for step, r in ((ACROSS, 0), (ALONG, 1), (ACROSS, 1), (ALONG, 0)):
-            piece_copy(step, time, mine[r]).start()
+            piece_copy(step, time, mine[r], r).start()
+
+    def share_start(time):
+        for q in mine:
+            piece_copy(CORE, time, q, 2).start()
 
     for mask in range(1, times):
         strength_copy(mask, me).start()
-    for q in other:
-        piece_copy(CORE, me, q).start()
+    for r, q in enumerate(other):
+        piece_copy(CORE, me, q, r).start()
 
     @pl.when(core == 0)
     def _():
         links_start(me)
 
-    for q in mine:
-        piece_copy(CORE, me, q).start()
+    share_start(me)
     loads[2].wait()
     row_ids = me * rows + lax.broadcasted_iota(jnp.int32, (rows, states), 0)
     column_ids = lax.broadcasted_iota(jnp.int32, (rows, states), 1)
@@ -312,8 +318,8 @@
     raiser[...] = jnp.where(live_columns, operator[...].astype(jnp.float32), 0.0).astype(
         jnp.bfloat16
     )
-    for q in mine:
-        piece_copy(CORE, partner, q).wait_recv()
+    for r, q in enumerate(mine):
+        piece_copy(CORE, partner, q, r).wait_recv()
 
     links_start(partner)
 
@@ -341,15 +347,22 @@
             down_copy(slot, time).start()
 
     def arrive(step, time, r):
-        piece_copy(step, time, mine[r]).wait_recv()
-        piece_copy(CORE, time, mine[r]).start()
+        piece_copy(step, time, mine[r], r).wait_recv()
+        piece_copy(CORE, time, mine[r], 2).start()
 
     def relay(step, time, r):
-        piece_copy(step, time, mine[r]).start()
+        piece_copy(step, time, mine[r], r).start()
 
     def shared(time):
-        for q in other:
-            piece_copy(CORE, time, q).wait_recv()
+        rest = history.at[time, pl.ds(0, states // 2)]
+        pltpu.make_async_remote_copy(
+            src_ref=rest,
+            dst_ref=rest,
+            send_sem=piece_send,
+            recv_sem=piece_recv.at[time, 2],
+            device_id={"tm": partner},
+            device_id_type=MESH,
+        ).wait_recv()
 
     order = [me, partner, x_even, y_even, x_even + 1, y_even + 1, d_even, d_even + 1]
     last = order[-1]
@@ -404,18 +417,27 @@
     live_rows = (row_ids < size) & (column_ids < size)
     shown = on_diagonal & (row_ids < size)
 
+    def wait_rows(buffer, send, recv, slots, step):
+        block = buffer.at[pl.ds(0, len(slots) * rows)]
+        pltpu.make_async_remote_copy(
+            src_ref=block,
+            dst_ref=block,
+            send_sem=send,
+            recv_sem=recv.at[signal_of(slots[0])],
+            device_id={"sector": sector + step},
+            device_id_type=MESH,
+        ).wait_recv()
+
     def combine(*slots):
         places = [row_block(order[slot]) for slot in slots]
 
         @pl.when(has_below)
         def _():
-            for slot in slots:
-                up_copy(slot, order[slot], -1).wait_recv()
+            wait_rows(below, up_send, up_recv, slots, -1)
 
         @pl.when(has_above)
         def _():
-            for slot in slots:
-                down_copy(slot, order[slot], 1).wait_recv()
+            wait_rows(above, down_send, down_recv, slots, 1)
 
         lowered = jnp.concatenate([above[place] for place in places], 0)
         downward = jnp.dot(lowered, operator[...], preferred_element_type=jnp.float32)
@@ -461,8 +483,7 @@
             out_ref[0, 0, row_block(me)] = fresh[moment]
 
     x_odd, y_odd = x_even + 1, y_even + 1
-    for mask in range(1, times):
-        strength_copy(mask, flipped(me, mask)).wait_recv()
+    strength_copy(CORE, 0, times - 1).wait_recv()
     both(2)
     both(3)
     combine(0, 1)
@@ -525,46 +546,47 @@
                 finish(d_even + moment)
             finish(d_even + moment + 1)
 
-    for mask in range(1, times):
+    strength_copy(CORE, 0, times - 1).wait_send()
+    blocks = history.at[pl.ds(0, times - 1)]
+    pltpu.make_async_remote_copy(
+        src_ref=blocks,
+        dst_ref=blocks,
+        send_sem=piece_send,
+        recv_sem=piece_recv.at[0, 0],
+        device_id={"tm": partner},
+        device_id_type=MESH,
+    ).wait_send()
+
+    def wait_sent(buffer, send, recv, step):
         pltpu.make_async_remote_copy(
-            src_ref=fresh.at[0],
-            dst_ref=out_ref.at[0, 0, row_block(flipped(me, mask))],
-            send_sem=out_send.at[0],
-            recv_sem=out_recv.at[flipped(me, mask)],
-            device_id={"tm": flipped(me, mask)},
-            device_id_type=MESH,
-        ).wait_recv()
-    for moment in range(times):
-
-        @pl.when((me != moment))
-        def _():
-            out_copy(moment, me).wait_send()
-
-    for mask in range(1, times):
-        strength_copy(mask, me).wait_send()
-    for q in mine + other:
-        piece_copy(CORE, me, q).wait_send()
-    for time in (even, even + 1):
-        for step in (ACROSS, ALONG):
-            for q in mine:
-                piece_copy(step, time, q).wait_send()
-    for parity in range(2):
-        for base in (x_even, y_even, d_even):
-            for q in mine:
-                piece_copy(CORE, base + parity, q).wait_send()
-        piece_copy(ALONG, x_even + parity, mine[0]).wait_send()
-        piece_copy(ACROSS, y_even + parity, mine[1]).wait_send()
+            src_ref=buffer,
+            dst_ref=buffer,
+            send_sem=send,
+            recv_sem=recv.at[0],
+            device_id={"sector": sector + step},
+            device_id_type=MESH,
+        ).wait_send()
 
     @pl.when(has_below)
     def _():
-        for slot in range(times):
-            down_copy(slot, order[slot]).wait_send()
+        wait_sent(down_rows, down_send, down_recv, -1)
 
     @pl.when(has_above)
     def _():
         turned_copy().wait_send()
-        for slot in range(times):
-            up_copy(slot, order[slot]).wait_send()
+        wait_sent(up_rows, up_send, up_recv, 1)
+
+    results = fresh.at[pl.ds(0, times - 1)]
+    leaving = pltpu.make_async_remote_copy(
+        src_ref=results,
+        dst_ref=results,
+        send_sem=out_send,
+        recv_sem=out_recv,
+        device_id={"tm": partner},
+        device_id_type=MESH,
+    )
+    leaving.wait_recv()
+    leaving.wait_send()
 
 
 def fused_device(propagator, rising_op, energies, hyb_particle, hyb_hole, sector_sizes):
@@ -604,16 +626,16 @@
             dma((6,)),
             dma,
             dma,
-            dma((times,)),
-            dma((times,)),
-            dma((times,)),
-            dma((times,)),
-            dma((3, times, PIECES)),
-            dma((times, PIECES)),
-            dma((times,)),
-            dma((times,)),
-            dma((times,)),
-            dma((times,)),
+            dma,
+            dma((times // 2 + 1,)),
+            dma,
+            dma((times // 2 + 1,)),
+            dma,
+            dma((times, 3)),
+            dma,
+            dma,
+            dma,
+            dma,
         ],
         compiler_params=pltpu.CompilerParams(
             collective_id=0, has_side_effects=True, vmem_limit_bytes=VMEM_GRANT

time: 52.4 us -> 50.9 us (0.971)
  Pallas kernels: 49.4 us -> 47.9 us
    pallas_call x1, Pallas kernels: 49.4 us -> 47.9 us  [fused_device(): pl.pallas_call(functools.partial(fused_kernel, times, lax.axis_size('sect...]
where the time goes in v3:
time: 50.9 us; the launch traced here: 50.8 us
  Pallas kernels  47.9 us (94%)
  between operations  1.97 us (4%)
  local copies, waits for them, and re-layouts  0.9 us (2%)
    pallas_call x1, Pallas kernels, fused_device(): pl.pallas_call(functools.partial(fused_kernel, times, lax.axis_size('sect...  47.9 us

profile of v3, /device:TPU:15, one launch (start us, length us, event | category | flops | bytes accessed | tf_op | source)
XLA Modules:
  0.0 50.8 jit_solution(4967252751935819279)
XLA Ops:
  0.0 0.0 copy-start
  2.0 0.0 copy-done
  2.0 47.9 %shard_map.64 = bf16[1,1,640,640]{3,2,1,0:T(8,128)(2,1)S(1)} custom-call(s32[1]{0:T(128)S(6)} %copy.10.size_hbm, f32[1]{0:T(128)S(6)} %copy.8.particle_hbm, f32[1]{0:T(128)S(6)} %copy.9.hole_hbm, bf16[1,1,640,640]{3,2,1,0:T(8,128)(2,1)} %prop_hbm.1, bf16[1,640,640]{2,1,0:T(8,128)(2,1)} %operator_hbm.1, f32[1,640]{1,0:T(1,128)S(1)} %copy-done), custom_call_target="tpu_custom_call" | custom-call | tf_op jit(solution)/shard_map/pallas_call | solution.py:600
  49.9 0.9 %copy.11 = bf16[1,1,640,640]{3,2,1,0:T(8,128)(2,1)} copy(bf16[1,1,640,640]{3,2,1,0:T(8,128)(2,1)S(1)} %shard_map.64) | data formatting | bytes 1638400
Async XLA Ops:
  0.0 2.0 %copy-start = (f32[1,640]{1,0:T(1,128)S(1)}, f32[1,640]{1,0:T(1,128)}, u32[]{:S(2)}) copy-start(f32[1,640]{1,0:T(1,128)} %energy_hbm.1) | copy-start | bytes 7684

commit v4 on v3

--- a/solution.py
+++ b/solution.py
@@ -503,8 +503,18 @@
     arrive(ACROSS, d_even, 1)
     convolve(even, x_odd)
     convolve(even, y_odd)
+
     both(6)
     accumulate(even, d_even)
+
+    @pl.when(even == 0)
+    def _():
+        sums[row_block(x_even)] += jnp.dot(
+            energy_in[row_block(x_even)], history[0], preferred_element_type=jnp.float32
+        )
+        for moment in range(times // 4 + 1):
+            finish(moment)
+
     arrive(ALONG, last, 0)
     arrive(ACROSS, last, 1)
     combine(4, 5)
@@ -512,30 +522,47 @@
     def finish_between(start, stop, allowed):
         for moment in range(start, stop, 2):
 
-            @pl.when(allowed & (moment < d_even))
+            @pl.when(allowed & (moment < d_even) & ((even != 0) | (moment > times // 4)))
             def _():
                 finish(moment)
+
+            @pl.when(allowed & (moment < d_even) & ((even != 0) | (moment + 1 > times // 4)))
+            def _():
                 finish(moment + 1)
 
     first_half = d_even >= times // 2
-    convolve(x_even, even, even + 1)
-    convolve(x_even, x_even, x_odd)
-    finish_between(0, times // 2, first_half)
-    convolve(y_even, y_even, y_odd)
-    finish_between(0, times // 2, jnp.logical_not(first_half))
+
+    def early(allowed):
+        @pl.when(allowed)
+        def _():
+            convolve(x_even, even, even + 1)
+            convolve(x_even, x_even, x_odd)
+            finish_between(0, times // 2, first_half)
+            convolve(y_even, y_even, y_odd)
+            finish_between(0, times // 2, jnp.logical_not(first_half))
+
+    early(even == 0)
     both(7)
+    early(even != 0)
+    convolve(x_even, d_even, last)
+    convolve(y_even, d_even, last)
+
+    def finish_next(allowed):
+        @pl.when(allowed)
+        def _():
+            combine(6)
+            sums[row_block(d_even)] += jnp.dot(
+                energy_in[row_block(d_even)], history[0], preferred_element_type=jnp.float32
+            )
+            finish(d_even)
+
+    finish_next(even != 0)
     accumulate(x_even, y_even, y_odd)
     accumulate(y_even, x_even, x_odd)
     convolve(y_even, even, even + 1)
     finish_between(times // 2, times, first_half)
     accumulate(even, last)
-    convolve(x_even, d_even, last)
-    convolve(y_even, d_even, last)
-    combine(6)
-    sums[row_block(d_even)] += jnp.dot(
-        energy_in[row_block(d_even)], history[0], preferred_element_type=jnp.float32
-    )
-    finish(d_even)
+    finish_next(even == 0)
     combine(7)
     for moment in range(0, times, 2):
 

time: 50.9 us -> 49.8 us (0.978)
  Pallas kernels: 47.9 us -> 46.8 us
    pallas_call x1, Pallas kernels: 47.9 us -> 46.8 us  [fused_device(): pl.pallas_call(functools.partial(fused_kernel, times, lax.axis_size('sect...]
where the time goes in v4:
time: 49.8 us; the launch traced here: 49.7 us
  Pallas kernels  46.8 us (94%)
  between operations  1.97 us (4%)
  local copies, waits for them, and re-layouts  0.9 us (2%)
    pallas_call x1, Pallas kernels, fused_device(): pl.pallas_call(functools.partial(fused_kernel, times, lax.axis_size('sect...  46.8 us

profile of v4, /device:TPU:15, one launch (start us, length us, event | category | flops | bytes accessed | tf_op | source)
XLA Modules:
  0.0 49.7 jit_solution(12684816748932817396)
XLA Ops:
  0.0 0.0 copy-start
  2.0 0.0 copy-done
  2.0 46.8 %shard_map.64 = bf16[1,1,640,640]{3,2,1,0:T(8,128)(2,1)S(1)} custom-call(s32[1]{0:T(128)S(6)} %copy.10.size_hbm, f32[1]{0:T(128)S(6)} %copy.8.particle_hbm, f32[1]{0:T(128)S(6)} %copy.9.hole_hbm, bf16[1,1,640,640]{3,2,1,0:T(8,128)(2,1)} %prop_hbm.1, bf16[1,640,640]{2,1,0:T(8,128)(2,1)} %operator_hbm.1, f32[1,640]{1,0:T(1,128)S(1)} %copy-done), custom_call_target="tpu_custom_call" | custom-call | tf_op jit(solution)/shard_map/pallas_call | solution.py:627
  48.8 0.9 %copy.11 = bf16[1,1,640,640]{3,2,1,0:T(8,128)(2,1)} copy(bf16[1,1,640,640]{3,2,1,0:T(8,128)(2,1)S(1)} %shard_map.64) | data formatting | bytes 1638400
Async XLA Ops:
  0.0 2.0 %copy-start = (f32[1,640]{1,0:T(1,128)S(1)}, f32[1,640]{1,0:T(1,128)}, u32[]{:S(2)}) copy-start(f32[1,640]{1,0:T(1,128)} %energy_hbm.1) | copy-start | bytes 7684

commit v5 on v4

--- a/solution.py
+++ b/solution.py
@@ -561,8 +561,8 @@
     accumulate(y_even, x_even, x_odd)
     convolve(y_even, even, even + 1)
     finish_between(times // 2, times, first_half)
+    finish_next(even == 0)
     accumulate(even, last)
-    finish_next(even == 0)
     combine(7)
     for moment in range(0, times, 2):
 

time: 49.8 us -> 49.6 us (level)
  no operation moved by 1% of the time
where the time goes in v5:
time: 49.6 us; the launch traced here: 49.4 us
  Pallas kernels  46.5 us (94%)
  between operations  1.97 us (4%)
  local copies, waits for them, and re-layouts  0.9 us (2%)
    pallas_call x1, Pallas kernels, fused_device(): pl.pallas_call(functools.partial(fused_kernel, times, lax.axis_size('sect...  46.5 us

profile of v5, /device:TPU:15, one launch (start us, length us, event | category | flops | bytes accessed | tf_op | source)
XLA Modules:
  0.0 49.4 jit_solution(7384172205553251129)
XLA Ops:
  0.0 0.0 copy-start
  2.0 0.0 copy-done
  2.0 46.5 %shard_map.64 = bf16[1,1,640,640]{3,2,1,0:T(8,128)(2,1)S(1)} custom-call(s32[1]{0:T(128)S(6)} %copy.10.size_hbm, f32[1]{0:T(128)S(6)} %copy.8.particle_hbm, f32[1]{0:T(128)S(6)} %copy.9.hole_hbm, bf16[1,1,640,640]{3,2,1,0:T(8,128)(2,1)} %prop_hbm.1, bf16[1,640,640]{2,1,0:T(8,128)(2,1)} %operator_hbm.1, f32[1,640]{1,0:T(1,128)S(1)} %copy-done), custom_call_target="tpu_custom_call" | custom-call | tf_op jit(solution)/shard_map/pallas_call | solution.py:627
  48.5 0.9 %copy.11 = bf16[1,1,640,640]{3,2,1,0:T(8,128)(2,1)} copy(bf16[1,1,640,640]{3,2,1,0:T(8,128)(2,1)S(1)} %shard_map.64) | data formatting | bytes 1638400
Async XLA Ops:
  0.0 2.0 %copy-start = (f32[1,640]{1,0:T(1,128)S(1)}, f32[1,640]{1,0:T(1,128)}, u32[]{:S(2)}) copy-start(f32[1,640]{1,0:T(1,128)} %energy_hbm.1) | copy-start | bytes 7684

commit v6 on v5

--- a/solution.py
+++ b/solution.py
@@ -298,6 +298,17 @@
         links_start(me)
 
     share_start(me)
+    piece_copy(CORE, partner, mine[0], 0).wait_recv()
+    piece_copy(ACROSS, partner, mine[0], 0).start()
+    piece_copy(CORE, partner, mine[1], 1).wait_recv()
+    piece_copy(ALONG, partner, mine[1], 1).start()
+    piece_copy(ACROSS, partner, mine[1], 1).start()
+    piece_copy(ALONG, partner, mine[0], 0).start()
+
+    @pl.when(core == 1)
+    def _():
+        links_start(me)
+
     loads[2].wait()
     row_ids = me * rows + lax.broadcasted_iota(jnp.int32, (rows, states), 0)
     column_ids = lax.broadcasted_iota(jnp.int32, (rows, states), 1)
@@ -318,15 +329,6 @@
     raiser[...] = jnp.where(live_columns, operator[...].astype(jnp.float32), 0.0).astype(
         jnp.bfloat16
     )
-    for r, q in enumerate(mine):
-        piece_copy(CORE, partner, q, r).wait_recv()
-
-    links_start(partner)
-
-    @pl.when(core == 1)
-    def _():
-        links_start(me)
-
     def product_of(left, time):
         return jnp.dot(left, history[time], preferred_element_type=jnp.float32)
 
@@ -542,6 +544,13 @@
             finish_between(0, times // 2, jnp.logical_not(first_half))
 
     early(even == 0)
+
+    def opposite(allowed):
+        @pl.when(allowed)
+        def _():
+            accumulate(x_even, y_even, y_odd)
+
+    opposite(even != 0)
     both(7)
     early(even != 0)
     convolve(x_even, d_even, last)
@@ -557,7 +566,7 @@
             finish(d_even)
 
     finish_next(even != 0)
-    accumulate(x_even, y_even, y_odd)
+    opposite(even == 0)
     accumulate(y_even, x_even, x_odd)
     convolve(y_even, even, even + 1)
     finish_between(times // 2, times, first_half)

time: 49.6 us -> 49.6 us (level)
  no operation moved by 1% of the time
where the time goes in v6:
time: 49.6 us; the launch traced here: 49.5 us
  Pallas kernels  46.6 us (94%)
  between operations  1.97 us (4%)
  local copies, waits for them, and re-layouts  0.9 us (2%)
    pallas_call x1, Pallas kernels, fused_device(): pl.pallas_call(functools.partial(fused_kernel, times, lax.axis_size('sect...  46.6 us

profile of v6, /device:TPU:15, one launch (start us, length us, event | category | flops | bytes accessed | tf_op | source)
XLA Modules:
  0.0 49.5 jit_solution(13573298811104618495)
XLA Ops:
  0.0 0.0 copy-start
  2.0 0.0 copy-done
  2.0 46.6 %shard_map.64 = bf16[1,1,640,640]{3,2,1,0:T(8,128)(2,1)S(1)} custom-call(s32[1]{0:T(128)S(6)} %copy.10.size_hbm, f32[1]{0:T(128)S(6)} %copy.8.particle_hbm, f32[1]{0:T(128)S(6)} %copy.9.hole_hbm, bf16[1,1,640,640]{3,2,1,0:T(8,128)(2,1)} %prop_hbm.1, bf16[1,640,640]{2,1,0:T(8,128)(2,1)} %operator_hbm.1, f32[1,640]{1,0:T(1,128)S(1)} %copy-done), custom_call_target="tpu_custom_call" | custom-call | tf_op jit(solution)/shard_map/pallas_call | solution.py:636
  48.6 0.9 %copy.11 = bf16[1,1,640,640]{3,2,1,0:T(8,128)(2,1)} copy(bf16[1,1,640,640]{3,2,1,0:T(8,128)(2,1)S(1)} %shard_map.64) | data formatting | bytes 1638400
Async XLA Ops:
  0.0 2.0 %copy-start = (f32[1,640]{1,0:T(1,128)S(1)}, f32[1,640]{1,0:T(1,128)}, u32[]{:S(2)}) copy-start(f32[1,640]{1,0:T(1,128)} %energy_hbm.1) | copy-start | bytes 7684
